TPU v7x, 256 devices: a whole 4x4x8 slice. The times are simulated.
256 devices in a mesh: row: 32 (over z, y_lo, core), col: 8 (over x, y_hi).
Axes of the slice: x: 4, y: 4 (y_hi: 2, y_lo: 2; y = y_hi * 2 + y_lo), z: 8, core: 2. Of those that a mesh axis runs over, the one named last changes fastest.
Arguments:
- activations: bfloat16 [1024, 16384], P('col', 'row'), may hold values from -6 to 6
- out_grad: bfloat16 [1024, 16384], P('col', 'row'), may hold values from -2 to 2
- gate_pre: bfloat16 [1024, 8192], P('row', 'col'), may hold values from -6 to 6
- up_pre: bfloat16 [1024, 8192], P('row', 'col'), may hold values from -6 to 6
- gate_weight: bfloat16 [16384, 8192], P('row', 'col'), may hold values from -0.046875 to 0.046875
- up_weight: bfloat16 [16384, 8192], P('row', 'col'), may hold values from -0.046875 to 0.046875
- down_weight: bfloat16 [8192, 16384], P('col', 'row'), may hold values from -0.0625 to 0.0625
Outputs:
- input_grad: bfloat16 [1024, 16384], P('col', 'row')
- gate_grad: bfloat16 [16384, 8192], P('row', 'col')
- up_grad: bfloat16 [16384, 8192], P('row', 'col')
- down_grad: bfloat16 [8192, 16384], P('col', 'row')
All inputs are finite; a program needn't handle non-finite values.
Results may differ from a plain program's by a relative error of at most 0.0051.
Values may be sent and summed in bfloat16 or wider, within the bound.
A program may use at most 64 MiB of HBM per device.

v0:
```python
import jax
import jax.numpy as jnp
from jax import lax
from jax.sharding import PartitionSpec as P


def contract_rows(left, right):
    return lax.dot_general(
        left, right, (((0,), (0,)), ((), ())), preferred_element_type=jnp.float32
    )


def contract_cols(left, right):
    return lax.dot_general(
        left, right, (((1,), (1,)), ((), ())), preferred_element_type=jnp.float32
    )


def derive(hidden_grad, gate_pre, up_pre):
    gate_val = gate_pre.astype(jnp.float32)
    up_val = up_pre.astype(jnp.float32)
    gate_sig = jax.nn.sigmoid(gate_val)
    swish_val = gate_val * gate_sig
    hidden = (swish_val * up_val).astype(jnp.bfloat16)
    gate_back = (hidden_grad * up_val * gate_sig * (1.0 + gate_val * (1.0 - gate_sig))).astype(
        jnp.bfloat16
    )
    up_back = (hidden_grad * swish_val).astype(jnp.bfloat16)
    return (hidden, gate_back, up_back)


def per_device(activations, out_grad, gate_pre, up_pre, gate_weight, up_weight, down_weight):
    acts_all, grad_all = (
        lax.all_gather(activations, "col", axis=0, tiled=True),
        lax.all_gather(out_grad, "col", axis=0, tiled=True),
    )
    grad_rows = grad_all
    hidden_grad = lax.psum_scatter(
        contract_cols(grad_rows, down_weight), "row", scatter_dimension=0, tiled=True
    )
    hidden, gate_back, up_back = derive(hidden_grad, gate_pre, up_pre)
    hid_piece = lax.all_gather(hidden, "row", axis=0, tiled=True)
    gate_piece = lax.all_gather(gate_back, "row", axis=0, tiled=True)
    up_piece = lax.all_gather(up_back, "row", axis=0, tiled=True)
    grad_rows = grad_all
    down_acc = contract_rows(hid_piece, grad_rows)
    gate_acc = contract_rows(acts_all, gate_piece)
    up_acc = contract_rows(acts_all, up_piece)
    input_rows = contract_cols(gate_piece, gate_weight) + contract_cols(up_piece, up_weight)
    input_acc = input_rows
    down_acc, gate_acc, up_acc, input_acc = (down_acc, gate_acc, up_acc, input_acc)
    input_grad = lax.psum_scatter(input_acc, "col", scatter_dimension=0, tiled=True)
    return (
        input_grad.astype(jnp.bfloat16),
        gate_acc.astype(jnp.bfloat16),
        up_acc.astype(jnp.bfloat16),
        down_acc.astype(jnp.bfloat16),
    )


def solution(mesh):
    placed = (
        P("col", "row"),
        P("col", "row"),
        P("row", "col"),
        P("row", "col"),
        P("row", "col"),
        P("row", "col"),
        P("col", "row"),
    )
    return jax.shard_map(
        per_device,
        mesh=mesh,
        in_specs=placed,
        out_specs=(P("col", "row"), P("row", "col"), P("row", "col"), P("col", "row")),
        check_vma=False,
    )
```

profile of v0, /device:TPU:32, one launch (start us, length us, event | category | flops | bytes accessed | tf_op | source)
XLA Modules:
  0.0 538.8 jit_solution(6172015009212809988)
XLA Ops:
  7.2 0.0 copy-start
  7.2 0.0 all-gather.6.cloned.1.call-start
  7.2 0.7 all-gather.6.cloned.1.call-update
  7.9 0.0 reduce-scatter.3.cloned.1.call-start
  8.0 57.5 %all-gather.6.cloned.1.call-done = bf16[1024,512]{1,0:T(8,128)(2,1)} async-done(((bf16[128,512]{1,0:T(8,128)(2,1)}), bf16[1024,512]{1,0:T(8,128)(2,1)}) %all-gather.6.cloned.1.call-update) | async-done | bytes 1048592 | tf_op jit(solution)/shard_map/all_gather | solution.py:35
  65.5 0.0 copy-done
  65.5 4.4 fusion.10
  69.9 0.0 copy-start.1
  69.9 0.0 copy-start.2
  70.0 0.0 copy-start.3
  70.0 0.0 reduce-scatter.3.cloned.1.call-update
  70.0 0.0 all-gather.8.cloned.1.call-start
  70.0 117.0 %reduce-scatter.3.cloned.1.call-done = f32[32,1024]{1,0:T(8,128)} async-done(((f32[1024,1024]{1,0:T(8,128)}), f32[32,1024]{1,0:T(8,128)}) %reduce-scatter.3.cloned.1.call-update) | async-done | bytes 131088 | tf_op jit(solution)/shard_map/reduce_scatter | solution.py:38
  187.1 0.0 copy-done.1
  187.1 0.0 copy-done.2
  187.1 1.6 multiply_convert_fusion
  188.7 0.0 all-gather.8.cloned.1.call-update
  188.7 0.0 all-gather.10.cloned.1.call-start
  188.8 0.5 all-gather.10.cloned.1.call-update
  189.3 0.0 all-gather.12.cloned.1.call-start
  189.4 0.5 all-gather.12.cloned.1.call-update
  189.9 0.0 all-gather.14.cloned.1.call-start
  189.9 0.5 all-gather.14.cloned.1.call-update
  190.5 0.0 copy-start.4
  190.5 0.0 reduce-scatter.5.cloned.1.call-start
  190.5 67.7 %all-gather.8.cloned.1.call-done = bf16[1024,1024]{1,0:T(8,128)(2,1)} async-done(((bf16[32,1024]{1,0:T(8,128)(2,1)}), bf16[1024,1024]{1,0:T(8,128)(2,1)}) %all-gather.8.cloned.1.call-update) | async-done | bytes 2097168 | tf_op jit(solution)/shard_map/all_gather | solution.py:43
  258.2 0.0 copy-done.3
  258.2 4.2 fusion.11
  262.5 62.1 %all-gather.10.cloned.1.call-done = bf16[1024,1024]{1,0:T(8,128)(2,1)} async-done(((bf16[32,1024]{1,0:T(8,128)(2,1)}), bf16[1024,1024]{1,0:T(8,128)(2,1)}) %all-gather.10.cloned.1.call-update) | async-done | bytes 2097168 | tf_op jit(solution)/shard_map/all_gather | solution.py:44
  324.5 0.0 copy-done.4
  324.5 4.9 convolution_add_fusion
  329.4 0.0 reduce-scatter.5.cloned.1.call-update
  329.5 50.4 %all-gather.12.cloned.1.call-done = bf16[1024,512]{1,0:T(8,128)(2,1)} async-done(((bf16[128,512]{1,0:T(8,128)(2,1)}), bf16[1024,512]{1,0:T(8,128)(2,1)}) %all-gather.12.cloned.1.call-update) | async-done | bytes 1048592 | tf_op jit(solution)/shard_map/all_gather | solution.py:34
  379.9 3.1 fusion
  383.0 0.0 copy-start.6
  383.0 1.3 copy.11
  384.3 0.0 copy-done.6
  384.3 2.9 fusion.1
  387.2 0.0 copy-start.5
  387.2 1.3 copy.12
  388.6 55.5 %all-gather.14.cloned.1.call-done = bf16[1024,1024]{1,0:T(8,128)(2,1)} async-done(((bf16[32,1024]{1,0:T(8,128)(2,1)}), bf16[1024,1024]{1,0:T(8,128)(2,1)}) %all-gather.14.cloned.1.call-update) | async-done | bytes 2097168 | tf_op jit(solution)/shard_map/all_gather | solution.py:42
  444.0 0.0 copy-done.5
  444.0 3.8 convolution_convert_fusion
  447.9 82.5 %reduce-scatter.5.cloned.1.call-done = f32[128,512]{1,0:T(8,128)} async-done(((f32[1024,512]{1,0:T(8,128)}), f32[128,512]{1,0:T(8,128)}) %reduce-scatter.5.cloned.1.call-update) | async-done | bytes 262160 | tf_op jit(solution)/shard_map/reduce_scatter | solution.py:52
  530.4 1.6 convert_element_type.37
Async XLA Ops:
  7.2 58.3 %copy-start = (bf16[1024,512]{1,0:T(8,128)(2,1)S(1)}, bf16[1024,512]{1,0:T(8,128)(2,1)}, u32[]{:S(2)}) copy-start(bf16[1024,512]{1,0:T(8,128)(2,1)} %param.13) | copy-start | bytes 3145732
  7.2 58.3 %all-gather.6.cloned.1.call-start = ((), (), s32[]{:S(2)}) async-start(), calls=%async_computation.2 | async-start | bytes 1179648 | tf_op jit(solution)/shard_map/all_gather | solution.py:35
  7.9 179.1 %reduce-scatter.3.cloned.1.call-start = ((), (), s32[]{:S(2)}) async-start(), calls=%async_computation.3 | async-start | bytes 4325376 | tf_op jit(solution)/shard_map/reduce_scatter | solution.py:38
  69.9 117.1 %copy-start.1 = (bf16[32,1024]{1,0:T(8,128)(2,1)S(1)}, bf16[32,1024]{1,0:T(8,128)(2,1)}, u32[]{:S(2)}) copy-start(bf16[32,1024]{1,0:T(8,128)(2,1)} %param.9) | copy-start | bytes 196612
  69.9 117.1 %copy-start.2 = (bf16[32,1024]{1,0:T(8,128)(2,1)S(1)}, bf16[32,1024]{1,0:T(8,128)(2,1)}, u32[]{:S(2)}) copy-start(bf16[32,1024]{1,0:T(8,128)(2,1)} %param.10) | copy-start | bytes 196612
  70.0 188.3 %copy-start.3 = (bf16[512,1024]{1,0:T(8,128)(2,1)S(1)}, bf16[512,1024]{1,0:T(8,128)(2,1)}, u32[]{:S(2)}) copy-start(bf16[512,1024]{1,0:T(8,128)(2,1)} %param.11) | copy-start | bytes 3145732
  70.0 188.2 %all-gather.8.cloned.1.call-start = ((), (), s32[]{:S(2)}) async-start(), calls=%async_computation.4 | async-start | bytes 2162688 | tf_op jit(solution)/shard_map/all_gather | solution.py:43
  188.7 135.8 %all-gather.10.cloned.1.call-start = ((), (), s32[]{:S(2)}) async-start(), calls=%async_computation.5 | async-start | bytes 2162688 | tf_op jit(solution)/shard_map/all_gather | solution.py:44
  189.3 190.6 %all-gather.12.cloned.1.call-start = ((), (), s32[]{:S(2)}) async-start(), calls=%async_computation.7 | async-start | bytes 1179648 | tf_op jit(solution)/shard_map/all_gather | solution.py:34
  189.9 254.2 %all-gather.14.cloned.1.call-start = ((), (), s32[]{:S(2)}) async-start(), calls=%async_computation.8 | async-start | bytes 2162688 | tf_op jit(solution)/shard_map/all_gather | solution.py:42
  190.5 134.1 %copy-start.4 = (bf16[512,1024]{1,0:T(8,128)(2,1)S(1)}, bf16[512,1024]{1,0:T(8,128)(2,1)}, u32[]{:S(2)}) copy-start(bf16[512,1024]{1,0:T(8,128)(2,1)} %param.12) | copy-start | bytes 3145732
  190.5 339.9 %reduce-scatter.5.cloned.1.call-start = ((), (), s32[]{:S(2)}) async-start(), calls=%async_computation.6 | async-start | bytes 2359296 | tf_op jit(solution)/shard_map/reduce_scatter | solution.py:52
  383.0 1.3 copy-start.6
  387.2 56.8 %copy-start.5 = (bf16[1024,512]{1,0:T(8,128)(2,1)S(1)}, bf16[1024,512]{1,0:T(8,128)(2,1)}, u32[]{:S(2)}) copy-start(bf16[1024,512]{1,0:T(8,128)(2,1)} %all-gather.6.cloned.1.call-done) | copy-start | bytes 3145732
Sparse Core Ops, SparseCore 0:
  10.6 54.8 all-gather.5
  70.1 116.9 reduce-scatter.2
  189.5 68.6 all-gather.7
  260.5 63.9 all-gather.9
  327.0 52.8 all-gather.11
  381.6 62.4 all-gather.13
  448.1 82.2 reduce-scatter.4
where the time goes:
time: 539 us
  waiting for transfers between devices  495 us (92%)
  matrix products  23.4 us (4%)
  between operations  14.2 us (3%)
    reduce_scatter x1, waiting for transfers between devices, per_device(): lax.psum_scatter(contract_cols(grad_rows, down_weight), 'row', scatter_di...  117 us
    reduce_scatter x1, waiting for transfers between devices, per_device(): lax.psum_scatter(input_acc, 'col', scatter_dimension=0, tiled=True)  82.5 us
    all_gather x1, waiting for transfers between devices, per_device(): gate_piece = lax.all_gather(gate_back, 'row', axis=0, tiled=True)  67.7 us
    all_gather x1, waiting for transfers between devices, per_device(): up_piece = lax.all_gather(up_back, 'row', axis=0, tiled=True)  62.1 us
    all_gather x1, waiting for transfers between devices, per_device(): lax.all_gather(out_grad, 'col', axis=0, tiled=True)  57.5 us
    all_gather x1, waiting for transfers between devices, per_device(): hid_piece = lax.all_gather(hidden, 'row', axis=0, tiled=True)  55.5 us
    all_gather x1, waiting for transfers between devices, per_device(): lax.all_gather(activations, 'col', axis=0, tiled=True)  50.4 us
    dot_general x3, matrix products, contract_cols(): lax.dot_general(left, right, (((1,), (1,)), ((), ())), preferred_element_...  13.6 us
  transfers between devices with their start and end apart: 7, of which 7 were waited for; matrix products, arithmetic and copies ran while one was open for 4% of the time, Pallas kernels for 0%

commit v1 on v0

--- a/solution.py
+++ b/solution.py
@@ -39,8 +39,11 @@
         contract_cols(grad_rows, down_weight), "row", scatter_dimension=0, tiled=True
     )
     hidden, gate_back, up_back = derive(hidden_grad, gate_pre, up_pre)
-    hid_piece = lax.all_gather(hidden, "row", axis=0, tiled=True)
-    gate_piece = lax.all_gather(gate_back, "row", axis=0, tiled=True)
+    hid_piece, gate_piece = jnp.split(
+        lax.all_gather(jnp.concatenate([hidden, gate_back], axis=1), "row", axis=0, tiled=True),
+        [hidden.shape[1]],
+        axis=1,
+    )
     up_piece = lax.all_gather(up_back, "row", axis=0, tiled=True)
     grad_rows = grad_all
     down_acc = contract_rows(hid_piece, grad_rows)

time: 539 us -> 476 us (0.88)
  waiting for transfers between devices: 495 us -> 431 us
    all_gather x2 -> x1, waiting for transfers between devices: 123 us -> 64.3 us  [per_device(): lax.all_gather(jnp.concatenate([hidden, gate_back], axis=1), 'row', axis=...]
    reduce_scatter x1, waiting for transfers between devices: 82.5 us -> 71.8 us  [per_device(): lax.psum_scatter(input_acc, 'col', scatter_dimension=0, tiled=True)]
    all_gather x1, waiting for transfers between devices: 62.1 us -> 67.9 us  [per_device(): up_piece = lax.all_gather(up_back, 'row', axis=0, tiled=True)]
  transfers between devices with their start and end apart: 7 -> 6, of which waited for: 7 -> 6; matrix products, arithmetic and copies ran while one was open for 4% -> 5% of each run, Pallas kernels for 0% -> 0%
where the time goes in v1:
time: 476 us; the launch traced here: 475 us
  waiting for transfers between devices  431 us (91%)
  matrix products  23.8 us (5%)
  between operations  14.1 us (3%)
    reduce_scatter x1, waiting for transfers between devices, per_device(): lax.psum_scatter(contract_cols(grad_rows, down_weight), 'row', scatter_di...  117 us
    reduce_scatter x1, waiting for transfers between devices, per_device(): lax.psum_scatter(input_acc, 'col', scatter_dimension=0, tiled=True)  71.8 us
    all_gather x1, waiting for transfers between devices, per_device(): up_piece = lax.all_gather(up_back, 'row', axis=0, tiled=True)  67.9 us
    all_gather x1, waiting for transfers between devices, per_device(): lax.all_gather(jnp.concatenate([hidden, gate_back], axis=1), 'row', axis=...  64.3 us
    all_gather x1, waiting for transfers between devices, per_device(): lax.all_gather(out_grad, 'col', axis=0, tiled=True)  57.5 us
    all_gather x1, waiting for transfers between devices, per_device(): lax.all_gather(activations, 'col', axis=0, tiled=True)  50.7 us
    dot_general x3, matrix products, contract_cols(): lax.dot_general(left, right, (((1,), (1,)), ((), ())), preferred_element_...  13.6 us
    dot_general x3, matrix products, contract_rows(): lax.dot_general(left, right, (((0,), (0,)), ((), ())), preferred_element_...  10.2 us
  transfers between devices with their start and end apart: 6, of which 6 were waited for; matrix products, arithmetic and copies ran while one was open for 5% of the time, Pallas kernels for 0%

profile of v1, /device:TPU:32, one launch (start us, length us, event | category | flops | bytes accessed | tf_op | source)
XLA Modules:
  0.0 475.3 jit_solution(4923595145288498146)
XLA Ops:
  7.2 0.0 copy-start
  7.2 0.0 all-gather.5.cloned.1.call-start
  7.2 0.7 all-gather.5.cloned.1.call-update
  7.9 0.0 reduce-scatter.3.cloned.1.call-start
  8.0 57.5 %all-gather.5.cloned.1.call-done = bf16[1024,512]{1,0:T(8,128)(2,1)} async-done(((bf16[128,512]{1,0:T(8,128)(2,1)}), bf16[1024,512]{1,0:T(8,128)(2,1)}) %all-gather.5.cloned.1.call-update) | async-done | bytes 1048592 | tf_op jit(solution)/shard_map/all_gather | solution.py:35
  65.5 0.0 copy-done
  65.5 4.5 fusion.27
  70.0 0.0 copy-start.1
  70.0 0.0 copy-start.2
  70.0 0.0 copy-start.3
  70.0 0.0 reduce-scatter.3.cloned.1.call-update
  70.0 0.0 all-gather.9.cloned.1.call-start
  70.1 117.1 %reduce-scatter.3.cloned.1.call-done = f32[32,1024]{1,0:T(8,128)} async-done(((f32[1024,1024]{1,0:T(8,128)}), f32[32,1024]{1,0:T(8,128)}) %reduce-scatter.3.cloned.1.call-update) | async-done | bytes 131088 | tf_op jit(solution)/shard_map/reduce_scatter | solution.py:38
  187.1 0.0 copy-done.1
  187.1 0.0 copy-done.2
  187.1 1.6 fusion.22
  188.7 0.0 all-gather.9.cloned.1.call-update
  188.8 0.0 all-gather.7.cloned.1.call-start
  188.8 0.7 pad_maximum_fusion
  189.5 0.0 all-gather.7.cloned.1.call-update
  189.5 0.0 all-gather.11.cloned.1.call-start
  189.5 0.5 all-gather.11.cloned.1.call-update
  190.1 0.0 copy-start.4
  190.1 0.0 reduce-scatter.5.cloned.1.call-start
  190.1 67.9 %all-gather.9.cloned.1.call-done = bf16[1024,1024]{1,0:T(8,128)(2,1)} async-done(((bf16[32,1024]{1,0:T(8,128)(2,1)}), bf16[1024,1024]{1,0:T(8,128)(2,1)}) %all-gather.9.cloned.1.call-update) | async-done | bytes 2097168 | tf_op jit(solution)/shard_map/all_gather | solution.py:47
  258.1 0.0 copy-done.3
  258.1 4.2 fusion.28
  262.3 64.3 %all-gather.7.cloned.1.call-done = bf16[1024,2048]{1,0:T(8,128)(2,1)} async-done(((bf16[32,2048]{1,0:T(8,128)(2,1)}), bf16[1024,2048]{1,0:T(8,128)(2,1)}) %all-gather.7.cloned.1.call-update) | async-done | bytes 4194320 | tf_op jit(solution)/shard_map/all_gather | solution.py:43
  326.6 0.0 copy-done.4
  326.6 4.9 %fusion.6 = f32[1024,512]{1,0:T(8,128)} fusion(f32[1024,512]{1,0:T(8,128)} %fusion.28, bf16[512,1024]{1,0:T(8,128)(2,1)S(1)} %copy-done.4, bf16[1024,2048]{1,0:T(8,128)(2,1)} %all-gather.7.cloned.1.call-done), kind=kOutput, calls=%fused_computation.6 | convolution fusion | flops 1074266112 | bytes 7340032 | tf_op jit(solution)/shard_map/dot_general | solution.py:14
  331.5 0.0 reduce-scatter.5.cloned.1.call-update
  331.5 50.7 %all-gather.11.cloned.1.call-done = bf16[1024,512]{1,0:T(8,128)(2,1)} async-done(((bf16[128,512]{1,0:T(8,128)(2,1)}), bf16[1024,512]{1,0:T(8,128)(2,1)}) %all-gather.11.cloned.1.call-update) | async-done | bytes 1048592 | tf_op jit(solution)/shard_map/all_gather | solution.py:34
  382.2 3.1 fusion.15
  385.3 1.3 copy.12
  386.6 0.0 copy-start.5
  386.6 3.2 fusion.16
  389.9 1.3 copy.11
  391.2 0.0 copy-done.5
  391.2 3.8 fusion.12
  395.0 71.8 %reduce-scatter.5.cloned.1.call-done = f32[128,512]{1,0:T(8,128)} async-done(((f32[1024,512]{1,0:T(8,128)}), f32[128,512]{1,0:T(8,128)}) %reduce-scatter.5.cloned.1.call-update) | async-done | bytes 262160 | tf_op jit(solution)/shard_map/reduce_scatter | solution.py:55
  466.8 1.6 convert_element_type.38
Async XLA Ops:
  7.2 58.3 %copy-start = (bf16[1024,512]{1,0:T(8,128)(2,1)S(1)}, bf16[1024,512]{1,0:T(8,128)(2,1)}, u32[]{:S(2)}) copy-start(bf16[1024,512]{1,0:T(8,128)(2,1)} %param.13) | copy-start | bytes 3145732
  7.2 58.3 %all-gather.5.cloned.1.call-start = ((), (), s32[]{:S(2)}) async-start(), calls=%async_computation.2 | async-start | bytes 1179648 | tf_op jit(solution)/shard_map/all_gather | solution.py:35
  7.9 179.2 %reduce-scatter.3.cloned.1.call-start = ((), (), s32[]{:S(2)}) async-start(), calls=%async_computation.3 | async-start | bytes 4325376 | tf_op jit(solution)/shard_map/reduce_scatter | solution.py:38
  70.0 117.1 %copy-start.1 = (bf16[32,1024]{1,0:T(8,128)(2,1)S(1)}, bf16[32,1024]{1,0:T(8,128)(2,1)}, u32[]{:S(2)}) copy-start(bf16[32,1024]{1,0:T(8,128)(2,1)} %param.10) | copy-start | bytes 196612
  70.0 117.1 %copy-start.2 = (bf16[32,1024]{1,0:T(8,128)(2,1)S(1)}, bf16[32,1024]{1,0:T(8,128)(2,1)}, u32[]{:S(2)}) copy-start(bf16[32,1024]{1,0:T(8,128)(2,1)} %param.9) | copy-start | bytes 196612
  70.0 188.1 %copy-start.3 = (bf16[512,1024]{1,0:T(8,128)(2,1)S(1)}, bf16[512,1024]{1,0:T(8,128)(2,1)}, u32[]{:S(2)}) copy-start(bf16[512,1024]{1,0:T(8,128)(2,1)} %param.12) | copy-start | bytes 3145732
  70.0 188.1 %all-gather.9.cloned.1.call-start = ((), (), s32[]{:S(2)}) async-start(), calls=%async_computation.5 | async-start | bytes 2162688 | tf_op jit(solution)/shard_map/all_gather | solution.py:47
  188.8 137.8 %all-gather.7.cloned.1.call-start = ((), (), s32[]{:S(2)}) async-start(), calls=%async_computation.4 | async-start | bytes 4325376 | tf_op jit(solution)/shard_map/all_gather | solution.py:43
  189.5 192.7 %all-gather.11.cloned.1.call-start = ((), (), s32[]{:S(2)}) async-start(), calls=%async_computation.7 | async-start | bytes 1179648 | tf_op jit(solution)/shard_map/all_gather | solution.py:34
  190.1 136.5 %copy-start.4 = (bf16[512,1024]{1,0:T(8,128)(2,1)S(1)}, bf16[512,1024]{1,0:T(8,128)(2,1)}, u32[]{:S(2)}) copy-start(bf16[512,1024]{1,0:T(8,128)(2,1)} %param.11) | copy-start | bytes 3145732
  190.1 276.7 %reduce-scatter.5.cloned.1.call-start = ((), (), s32[]{:S(2)}) async-start(), calls=%async_computation.6 | async-start | bytes 2359296 | tf_op jit(solution)/shard_map/reduce_scatter | solution.py:55
  386.6 4.5 copy-start.5
Sparse Core Ops, SparseCore 0:
  10.6 54.8 all-gather.4
  70.1 116.9 reduce-scatter.2
  189.5 68.4 all-gather.8
  260.4 66.1 all-gather.6
  329.1 53.0 all-gather.10
  386.1 80.6 reduce-scatter.4
